TPU v7x, 32 devices: a whole 2x2x4 slice. The times are simulated.
32 devices in a mesh: lat: 8 (over y, x, core), lon: 4 (over z).
Axes of the slice: x: 2, y: 2, z: 4, core: 2. Of those that a mesh axis runs over, the one named last changes fastest.
Arguments:
- tracers: float32 [4, 4, 256, 720], P(None, None, 'lat', 'lon'), may hold values from -6 to 6
- courant: float32 [2, 4, 256, 720], P(None, None, 'lat', 'lon'), may hold values from -0.8 to 0.8
- cutoffs: int32 [256], replicated, may hold values from 1 to 360, as said below
Outputs:
- updated: float32 [4, 4, 256, 720], P(None, None, 'lat', 'lon')
- filtered_zonal: float32 [4, 256, 720], P(None, 'lat', 'lon')
Inputs may be any that keep to these rules, and one draw needn't show every extreme that they name: cutoffs[j] is 360 for every row j with min(j, 255 - j) >= 64, below 360 for all other rows, and 1 at the two pole rows.
All inputs are finite; a program needn't handle non-finite values.
Results may differ from a plain program's by a relative error of at most 0.0003.
Values sent between devices are 32-bit elements; how exact they have to be, the bound alone decides.
A program may use at most 64 MiB of HBM per device.

v0:
```python
import math
import jax
import numpy as np
import jax.numpy as jnp
from jax import lax
from jax.sharding import PartitionSpec as P


def padded(cells, sides, width, closed):
    for axis, dim in sides:
        count = lax.axis_size(axis)
        ends = count if closed else count - 1
        head = lax.slice_in_dim(cells, 0, width, axis=dim)
        tail = lax.slice_in_dim(cells, cells.shape[dim] - width, cells.shape[dim], axis=dim)
        cells = jnp.concatenate(
            [
                lax.ppermute(tail, axis, [(i, (i + 1) % count) for i in range(ends)]),
                cells,
                lax.ppermute(head, axis, [((i + 1) % count, i) for i in range(ends)]),
            ],
            axis=dim,
        )
    return cells


def take_range(values, start, count, axis_index):
    return lax.slice_in_dim(values, start, start + count, axis=axis_index)


def ppm_flux(extended, courant_faces, axis_index):
    cell_count = extended.shape[axis_index] - 6
    edge_values = 7.0 / 12.0 * (
        take_range(extended, 1, cell_count + 3, axis_index)
        + take_range(extended, 2, cell_count + 3, axis_index)
    ) - 1.0 / 12.0 * (
        take_range(extended, 0, cell_count + 3, axis_index)
        + take_range(extended, 3, cell_count + 3, axis_index)
    )
    left_edge = take_range(edge_values, 0, cell_count + 2, axis_index)
    right_edge = take_range(edge_values, 1, cell_count + 2, axis_index)
    centre = take_range(extended, 2, cell_count + 2, axis_index)
    slopes = right_edge - left_edge
    curvature = 6.0 * centre - 3.0 * (left_edge + right_edge)
    upwind = take_range(right_edge, 0, cell_count + 1, axis_index) - 0.5 * courant_faces * (
        take_range(slopes, 0, cell_count + 1, axis_index)
        - (1.0 - courant_faces * (2.0 / 3.0)) * take_range(curvature, 0, cell_count + 1, axis_index)
    )
    downwind = take_range(left_edge, 1, cell_count + 1, axis_index) - 0.5 * courant_faces * (
        take_range(slopes, 1, cell_count + 1, axis_index)
        + (1.0 + courant_faces * (2.0 / 3.0)) * take_range(curvature, 1, cell_count + 1, axis_index)
    )
    return courant_faces * jnp.where(courant_faces > 0, upwind, downwind)


def metric_weights(first_row, row_count, grid_rows):
    faces = first_row + jnp.arange(-1, row_count, dtype=jnp.int32)
    centres = first_row + jnp.arange(row_count, dtype=jnp.int32)
    face_weight = jnp.sin(
        jnp.minimum(faces + 1, grid_rows - 1 - faces).astype(jnp.float32) * (math.pi / grid_rows)
    )
    cell_weight = jnp.sin(
        (jnp.minimum(centres, grid_rows - 1 - centres).astype(jnp.float32) + 0.5)
        * (math.pi / grid_rows)
    )
    return (face_weight, cell_weight)


def angle_table(first_ids, second_ids, period):
    product = first_ids[:, None] * second_ids[None, :] % period
    angles = product.astype(jnp.float32) * (2.0 * math.pi / period)
    return (jnp.cos(angles), jnp.sin(angles))


def spectral_lowpass(row_block, limits, outer_count):
    row_count, circle = row_block.shape
    inner_count = circle // outer_count
    highest = lax.Precision.HIGHEST
    grid_values = row_block.reshape(row_count, outer_count, inner_count)
    outer_ids = jnp.arange(outer_count, dtype=jnp.int32)
    inner_ids = jnp.arange(inner_count, dtype=jnp.int32)
    outer_cos, outer_sin = angle_table(outer_ids, outer_ids, outer_count)
    inner_cos, inner_sin = angle_table(inner_ids, inner_ids, inner_count)
    twiddle_cos, twiddle_sin = angle_table(inner_ids, outer_ids, circle)
    first_real = jnp.einsum("rab,ak->rbk", grid_values, outer_cos, precision=highest)
    first_imag = -jnp.einsum("rab,ak->rbk", grid_values, outer_sin, precision=highest)
    turned_real = first_real * twiddle_cos + first_imag * twiddle_sin
    turned_imag = first_imag * twiddle_cos - first_real * twiddle_sin
    coeff_real = jnp.einsum("rbk,bj->rjk", turned_real, inner_cos, precision=highest) + jnp.einsum(
        "rbk,bj->rjk", turned_imag, inner_sin, precision=highest
    )
    coeff_imag = jnp.einsum("rbk,bj->rjk", turned_imag, inner_cos, precision=highest) - jnp.einsum(
        "rbk,bj->rjk", turned_real, inner_sin, precision=highest
    )
    wavenumber = inner_ids[:, None] * outer_count + outer_ids[None, :]
    folded = jnp.minimum(wavenumber, circle - wavenumber)
    keep_mask = folded[None, :, :] <= limits[:, None, None]
    coeff_real = jnp.where(keep_mask, coeff_real, 0.0)
    coeff_imag = jnp.where(keep_mask, coeff_imag, 0.0)
    back_real = jnp.einsum("rjk,jb->rbk", coeff_real, inner_cos, precision=highest) - jnp.einsum(
        "rjk,jb->rbk", coeff_imag, inner_sin, precision=highest
    )
    back_imag = jnp.einsum("rjk,jb->rbk", coeff_imag, inner_cos, precision=highest) + jnp.einsum(
        "rjk,jb->rbk", coeff_real, inner_sin, precision=highest
    )
    reverted_real = back_real * twiddle_cos - back_imag * twiddle_sin
    reverted_imag = back_imag * twiddle_cos + back_real * twiddle_sin
    signal = jnp.einsum("rbk,ka->rab", reverted_real, outer_cos, precision=highest) - jnp.einsum(
        "rbk,ka->rab", reverted_imag, outer_sin, precision=highest
    )
    return (signal / circle).reshape(row_count, circle)


def dense_tables(circle):
    half = circle // 2
    cell_ids = np.arange(circle, dtype=np.int64)
    cos_ids = np.arange(half + 1, dtype=np.int64)
    sin_ids = np.arange(1, half, dtype=np.int64)
    forward = np.concatenate(
        [
            np.cos(2.0 * np.pi * (cell_ids[:, None] * cos_ids[None, :] % circle) / circle),
            np.sin(2.0 * np.pi * (cell_ids[:, None] * sin_ids[None, :] % circle) / circle),
        ],
        axis=1,
    )
    out_ids = np.arange(-1, circle, dtype=np.int64)
    cos_scale = np.where((cos_ids == 0) | (cos_ids == half), 1.0, 2.0) / circle
    inverse = np.concatenate(
        [
            cos_scale[:, None]
            * np.cos(2.0 * np.pi * (cos_ids[:, None] * out_ids[None, :] % circle) / circle),
            2.0
            / circle
            * np.sin(2.0 * np.pi * (sin_ids[:, None] * out_ids[None, :] % circle) / circle),
        ],
        axis=0,
    )
    wavenumber = np.concatenate([cos_ids, sin_ids]).astype(np.int32)
    return (
        jnp.asarray(forward.astype(np.float32)),
        jnp.asarray(inverse.astype(np.float32)),
        jnp.asarray(wavenumber),
    )


def dense_lowpass(row_block, limits):
    circle = row_block.shape[1]
    forward, inverse, wavenumber = dense_tables(circle)
    highest = lax.Precision.HIGHEST
    coeff = jnp.dot(row_block, forward, precision=highest)
    coeff = jnp.where(wavenumber[None, :] <= limits[:, None], coeff, 0.0)
    return jnp.dot(coeff, inverse, precision=highest)


def circle_filter(row_block, limits, lon_groups):
    row_count, block_cols = row_block.shape
    whole_rows = lax.all_to_all(row_block, "lon", split_axis=0, concat_axis=1, tiled=True)
    circle = whole_rows.shape[1]
    held_count = row_count // lon_groups
    row_limits = lax.dynamic_slice_in_dim(limits, lax.axis_index("lon") * held_count, held_count)
    whole_ext = jnp.concatenate([whole_rows[:, -1:], whole_rows], axis=1)
    if circle <= 2048:
        lowpass_ext = dense_lowpass(whole_rows, row_limits)
    else:
        lowpass = spectral_lowpass(whole_rows, row_limits, lon_groups)
        lowpass_ext = jnp.concatenate([lowpass[:, -1:], lowpass], axis=1)
    lowpass_ext = jnp.where((row_limits < circle // 2)[:, None], lowpass_ext, whole_ext)
    slabs = jnp.stack(
        [lowpass_ext[:, k * block_cols : (k + 1) * block_cols + 1] for k in range(lon_groups)],
        axis=0,
    )
    back = lax.all_to_all(slabs, "lon", split_axis=0, concat_axis=1, tiled=True)
    return back.reshape(row_count, block_cols + 1)


def body(tracers, courant, cutoffs):
    levels, tracer_count, lat_rows, lon_cols = tracers.shape
    lon_groups = lax.axis_size("lon")
    lat_bands = lax.axis_size("lat")
    band_index = lax.axis_index("lat")
    grid_rows = lat_rows * lat_bands
    zonal = courant[0]
    meridional = courant[1]
    lat_stack = jnp.concatenate([tracers, meridional[:, None]], axis=1)
    lat_ext = padded(lat_stack, (("lat", 2),), 3, False)
    lon_ext = padded(tracers, (("lon", 3),), 3, True)
    flat_count = levels * lat_rows
    flat_zonal = zonal.reshape(flat_count, lon_cols)
    local_limits = lax.dynamic_slice_in_dim(cutoffs, band_index * lat_rows, lat_rows)
    filtered_flat = circle_filter(flat_zonal, jnp.tile(local_limits, levels), lon_groups)
    zonal_faces = filtered_flat.reshape(levels, 1, lat_rows, lon_cols + 1)
    filtered_zonal = zonal_faces[:, 0, :, 1:]
    flux_east = ppm_flux(lon_ext, zonal_faces, 3)
    face_weight, cell_weight = metric_weights(band_index * lat_rows, lat_rows, grid_rows)
    flux_north = (
        ppm_flux(lat_ext[:, :tracer_count], lat_ext[:, tracer_count:, 2 : lat_rows + 3, :], 2)
        * face_weight[None, None, :, None]
    )
    change = (
        flux_east[:, :, :, 1:]
        - flux_east[:, :, :, :-1]
        + (flux_north[:, :, 1:, :] - flux_north[:, :, :-1, :]) / cell_weight[None, None, :, None]
    )
    return (tracers - change, filtered_zonal)


def solution(mesh):
    in_specs = (P(None, None, "lat", "lon"), P(None, None, "lat", "lon"), P())
    out_specs = (P(None, None, "lat", "lon"), P(None, "lat", "lon"))
    return jax.shard_map(body, mesh=mesh, in_specs=in_specs, out_specs=out_specs, check_vma=False)
```

profile of v0, /device:TPU:0, one launch (start us, length us, event | category | flops | bytes accessed | tf_op | source)
XLA Modules:
  0.0 59.9 jit_solution(7719575748991586604)
XLA Ops:
  0.6 0.0 copy-start
  0.6 0.0 copy-start.10
  0.7 1.7 %slice_bitcast_fusion.2 = (f32[4,32,180]{2,1,0:T(8,128)}, f32[4,1,32,180]{3,2,1,0:T(8,128)S(1)}) fusion(f32[2,4,32,180]{3,2,1,0:T(8,128)} %param.7), kind=kLoop, calls=%fused_computation.59 | loop fusion | bytes 368640 | tf_op jit(solution)/shard_map/all_to_all | solution.py:156
  2.4 1.1 %pad_maximum_fusion.9 = (f32[4,5,3,180]{3,2,1,0:T(4,128)S(1)}, f32[4,5,3,180]{3,2,1,0:T(4,128)S(1)}) fusion(f32[4,1,32,180]{3,2,1,0:T(8,128)S(1)} %get-tuple-element.15, f32[4,4,32,180]{3,2,1,0:T(8,128)} %param.6), kind=kLoop, calls=%fused_computation.63 | loop fusion | flops 21600 | bytes 547200 | tf_op jit(solution)/shard_map/slice | solution.py:14
  3.4 1.3 %collective-permute-start.3 = (f32[4,5,3,180]{3,2,1,0:T(4,128)S(1)}, f32[4,5,3,180]{3,2,1,0:T(4,128)S(1)}, u32[]{:S(2)}, u32[]{:S(2)}) collective-permute-start(f32[4,5,3,180]{3,2,1,0:T(4,128)S(1)} %get-tuple-element.9), channel_id=1, source_target_pairs={{4,0},{8,4},{12,8},{16,12},{20,16},{24,20},{28,24},{5,1},{9,5},{13... | collective-permute-start | bytes 129608 | tf_op jit(solution)/shard_map/ppermute | solution.py:19
  4.7 3.0 %collective-permute-start.2 = (f32[4,5,3,180]{3,2,1,0:T(4,128)S(1)}, f32[4,5,3,180]{3,2,1,0:T(4,128)S(1)}, u32[]{:S(2)}, u32[]{:S(2)}) collective-permute-start(f32[4,5,3,180]{3,2,1,0:T(4,128)S(1)} %get-tuple-element.8), channel_id=1, source_target_pairs={{0,4},{4,8},{8,12},{12,16},{16,20},{20,24},{24,28},{1,5},{5,9},{9,... | collective-permute-start | bytes 129608 | tf_op jit(solution)/shard_map/ppermute | solution.py:17
  7.8 1.2 %fusion.34 = (f32[4,4,32,3]{3,2,1,0:T(8,128)S(1)}, f32[4,4,32,3]{3,2,1,0:T(8,128)S(1)}) fusion(f32[4,4,32,180]{3,2,1,0:T(8,128)} %param.6), kind=kLoop, calls=%fused_computation.77 | loop fusion | bytes 24576 | tf_op jit(solution)/shard_map/slice | solution.py:14
  8.9 5.1 %collective-permute-start.1 = (f32[4,4,32,3]{3,2,1,0:T(8,128)S(1)}, f32[4,4,32,3]{3,2,1,0:T(8,128)S(1)}, u32[]{:S(2)}, u32[]{:S(2)}) collective-permute-start(f32[4,4,32,3]{3,2,1,0:T(8,128)S(1)} %get-tuple-element.13), channel_id=1, source_target_pairs={{1,0},{2,1},{3,2},{0,3},{5,4},{6,5},{7,6},{4,7},{9,8},{10,9},{11,1... | collective-permute-start | bytes 18440 | tf_op jit(solution)/shard_map/ppermute | solution.py:19
  14.1 0.0 collective-permute-start
  14.1 5.1 %all-to-all-start = ((f32[4,32,180]{2,1,0:T(8,128)}), f32[4,32,180]{2,1,0:T(8,128)}, u32[]{:S(2)}, u32[]{:S(2)}) async-start(f32[4,32,180]{2,1,0:T(8,128)} %get-tuple-element.14), calls=%async_computation | async-start | bytes 262144 | tf_op jit(solution)/shard_map/all_to_all | solution.py:156
  19.2 0.1 dynamic_slice.6
  19.3 0.1 tile.10
  19.4 0.1 broadcast_compare_fusion.1
  19.5 0.6 fusion.33
  20.0 0.6 %collective-permute-done.1 = f32[4,4,32,3]{3,2,1,0:T(8,128)S(1)} collective-permute-done((f32[4,4,32,3]{3,2,1,0:T(8,128)S(1)}, f32[4,4,32,3]{3,2,1,0:T(8,128)S(1)}, u32[]{:S(2)}, u32[]{:S(2)}) %collective-permute-start.1) | collective-permute-done | bytes 6176 | tf_op jit(solution)/shard_map/ppermute | solution.py:19
  20.7 6.6 %collective-permute-done = f32[4,4,32,3]{3,2,1,0:T(8,128)S(1)} collective-permute-done((f32[4,4,32,3]{3,2,1,0:T(8,128)S(1)}, f32[4,4,32,3]{3,2,1,0:T(8,128)S(1)}, u32[]{:S(2)}, u32[]{:S(2)}) %collective-permute-start) | collective-permute-done | bytes 6176 | tf_op jit(solution)/shard_map/ppermute | solution.py:17
  27.2 0.0 copy-done
  27.2 0.3 pad_maximum_fusion.5
  27.5 0.6 fusion.28
  28.1 1.1 %slice_subtract_fusion.3 = (f32[4,4,32,182]{3,2,1,0:T(8,128)S(1)}, f32[4,4,32,182]{3,2,1,0:T(8,128)}) fusion(f32[4,4,32,183]{3,2,1,0:T(8,128)S(1)} %fusion.28, f32[4,4,32,186]{3,2,1,0:T(8,128)S(1)} %pad_maximum_fusion.5), kind=kLoop, calls=%fused_computation.50 | loop fusion | flops 465920 | bytes 1863680 | tf_op jit(solution)/shard_map/sub | solution.py:42
  29.2 0.0 collective-permute-done.3
  29.2 0.0 collective-permute-done.2
  29.2 0.1 pad_maximum_fusion
  29.3 0.0 copy-done.2
  29.4 0.5 copy-done.6
  29.8 0.3 fusion.13
  30.1 0.0 copy-start.8
  30.2 0.2 slice_subtract_fusion
  30.4 0.7 %copy-done.3 = f32[4,1,32,180]{3,2,1,0:T(8,128)S(1)} copy-done((f32[4,1,32,180]{3,2,1,0:T(8,128)S(1)}, f32[4,1,32,180]{3,2,1,0:T(8,128)}, u32[]{:S(2)}) %copy-start.3) | copy-done | bytes 92184
  31.0 0.0 copy-done.7
  31.1 0.7 %compare_bitcast_fusion = (pred[4,33,180]{2,1,0:T(8,128)(4,1)}, f32[4,1,33,180]{3,2,1,0:T(8,128)}) fusion(f32[4,1,32,180]{3,2,1,0:T(8,128)S(1)} %copy-done.3, f32[4,4,32,180]{3,2,1,0:T(8,128)S(1)} %copy-done, f32[4,5,3,180]{3,2,1,0:T(4,128)S(1)} %copy-done.7), kind=kLoop, calls=%fused_computation.55 | loop fusion | flops 71280 | bytes 622800 | tf_op jit(solution)/shard_map/jit(_where)/broadcast_in_dim | solution.py:52
  31.8 1.7 %multiply_bitcast_fusion = (f32[4,33,180]{2,1,0:T(8,128)}, f32[4,33,180]{2,1,0:T(8,128)}, f32[4,33,180]{2,1,0:T(8,128)}) fusion(f32[4,1,33,180]{3,2,1,0:T(8,128)} %get-tuple-element.5), kind=kLoop, calls=%fused_computation.54 | loop fusion | flops 95040 | bytes 380160 | tf_op jit(solution)/shard_map/mul | solution.py:44
  33.5 0.0 all-to-all-done
  33.5 1.6 %copy.8 = f32[32,4,180]{2,1,0:T(4,128)} copy(f32[32,4,180]{2,0,1:T(8,128)} %bitcast.1) | data formatting | bytes 184320 | tf_op jit(solution)/shard_map/all_to_all | solution.py:156
  35.2 1.7 %all_to_all.26 = f32[32,720]{1,0:T(8,128)} reshape(f32[32,4,180]{2,1,0:T(4,128)} %copy.8) | data formatting | bytes 184320 | tf_op jit(solution)/shard_map/all_to_all | solution.py:156
  36.9 0.9 %slice.175 = f32[32,1]{1,0:T(8,128)S(1)} slice(f32[32,720]{1,0:T(8,128)} %all_to_all.26), slice={[0:32], [719:720]} | slice | bytes 256 | tf_op jit(solution)/shard_map/slice | solution.py:160
  37.8 3.0 %fusion = f32[32,720]{1,0:T(8,128)S(1)} fusion(f32[720,720]{1,0:T(8,128)} %constant.14.clone, f32[32,720]{1,0:T(8,128)} %all_to_all.26, s32[720]{0:T(1024)S(1)} %copy-done.8, s32[32]{0:T(128)S(1)} %get-tuple-element.3), kind=kOutput, calls=%fused_computation.2 | convolution fusion | flops 199111680 | bytes 2260928 | tf_op jit(solution)/shard_map/dot_general | solution.py:149
  40.8 1.4 %convolution_select_fusion = f32[32,721]{1,0:T(8,128)S(1)} fusion(f32[32,720]{1,0:T(8,128)S(1)} %fusion, f32[720,721]{1,0:T(8,128)S(1)} %copy-done.4, f32[32,720]{1,0:T(8,128)S(1)} %copy-done.5, f32[32,1]{1,0:T(8,128)S(1)} %slice.175, pred[32]{0:T(512)(128)(4,1)S(1)} %get-tuple-element.2), kind=kOutput, calls=%fused_computation | convolution fusion | flops 199388224 | bytes 2353248 | tf_op jit(solution)/shard_map/dot_general | solution.py:151
  42.2 0.1 slice_bitcast_fusion.6
  42.3 0.7 %pad_maximum_fusion.7 = f32[4,32,181]{2,1,0:T(8,128)} fusion(f32[1,32,181]{2,1,0:T(8,128)S(1)} %get-tuple-element.23, f32[1,32,181]{2,1,0:T(8,128)S(1)} %get-tuple-element.24, f32[1,32,181]{2,1,0:T(8,128)S(1)} %get-tuple-element.25, f32[1,32,181]{2,1,0:T(8,128)S(1)} %get-tuple-element.22), kind=kLoop, calls=%fused_computation.57 | loop fusion | flops 69504 | bytes 185344 | tf_op jit(solution)/shard_map/stack | solution.py:167
  42.9 4.0 %all-to-all-start.1 = ((f32[4,32,181]{2,1,0:T(8,128)}), f32[4,32,181]{2,1,0:T(8,128)}, u32[]{:S(2)}, u32[]{:S(2)}) async-start(f32[4,32,181]{2,1,0:T(8,128)} %pad_maximum_fusion.7), calls=%async_computation.1 | async-start | bytes 262144 | tf_op jit(solution)/shard_map/all_to_all | solution.py:171
  46.9 2.4 %fusion.6 = f32[4,4,33,180]{3,2,1,0:T(8,128)} fusion(f32[4,4,34,180]{3,2,1,0:T(8,128)S(1)} %get-tuple-element.7, f32[4,4,34,180]{3,2,1,0:T(8,128)S(1)} %get-tuple-element.6, f32[4,4,35,180]{3,2,1,0:T(8,128)S(1)} %fusion.13, f32[33]{0:T(128)S(1)} %multiply_sine_fusion, f32[4,33,180]{2,1,0:T(8,128)} %get-tuple-element.18, f32[4,33,180]{2,1,0:T(8,128)} %get-tuple-element.17, ...), kind=kLoop, calls=%fused_computation.10 | loop fusion | flops 1045440 | bytes 2685012 | tf_op jit(solution)/shard_map/mul | solution.py:195
  49.3 4.2 %all-to-all-done.1 = f32[4,32,181]{2,1,0:T(8,128)} async-done(((f32[4,32,181]{2,1,0:T(8,128)}), f32[4,32,181]{2,1,0:T(8,128)}, u32[]{:S(2)}, u32[]{:S(2)}) %all-to-all-start.1) | async-done | bytes 92704 | tf_op jit(solution)/shard_map/all_to_all | solution.py:171
  53.5 1.7 %slice_bitcast_fusion = f32[4,32,180]{2,1,0:T(8,128)} fusion(f32[4,1,32,181]{3,2,0,1:T(8,128)} %bitcast.13), kind=kLoop, calls=%fused_computation.56 | loop fusion | bytes 184320 | tf_op jit(solution)/shard_map/squeeze | solution.py:191
  55.2 1.0 %broadcast_multiply_fusion = (f32[4,32,181]{2,1,0:T(8,128)S(1)}, f32[4,32,181]{2,1,0:T(8,128)S(1)}, f32[4,32,181]{2,1,0:T(8,128)S(1)}) fusion(f32[4,32,181]{2,1,0:T(8,128)} %all-to-all-done.1), kind=kLoop, calls=%fused_computation.64 | loop fusion | flops 92672 | bytes 370688 | tf_op jit(solution)/shard_map/mul | solution.py:44
  56.2 0.9 %broadcast_compare_fusion = pred[4,32,181]{2,1,0:T(8,128)(4,1)S(1)} fusion(f32[4,32,181]{2,1,0:T(8,128)} %all-to-all-done.1), kind=kLoop, calls=%fused_computation.65 | loop fusion | flops 23168 | bytes 115840 | tf_op jit(solution)/shard_map/gt | solution.py:52
  57.1 1.8 %fusion.22 = f32[4,4,32,181]{3,2,1,0:T(8,128)S(1)} fusion(f32[4,4,32,182]{3,2,1,0:T(8,128)} %get-tuple-element.11, f32[4,4,32,182]{3,2,1,0:T(8,128)S(1)} %get-tuple-element.10, f32[4,4,32,183]{3,2,1,0:T(8,128)S(1)} %fusion.28, f32[4,32,181]{2,1,0:T(8,128)S(1)} %get-tuple-element.20, f32[4,32,181]{2,1,0:T(8,128)S(1)} %get-tuple-element.21, ...), kind=kLoop, calls=%fused_computation.37 | loop fusion | flops 926720 | bytes 2617984 | tf_op jit(solution)/shard_map/mul | solution.py:52
  58.9 1.0 %fusion.17 = f32[4,4,32,180]{3,2,1,0:T(8,128)} fusion(f32[4,4,32,180]{3,2,1,0:T(8,128)S(1)} %copy-done, f32[4,4,33,180]{3,2,1,0:T(8,128)S(1)} %copy-done.1, f32[4,4,32,181]{3,2,1,0:T(8,128)S(1)} %fusion.22, f32[32]{0:T(128)S(1)} %copy-done.9), kind=kLoop, calls=%fused_computation.30 | loop fusion | flops 460800 | bytes 2211968 | tf_op jit(solution)/shard_map/sub | solution.py:203
  (16 shorter events, 0.1 us)
Async XLA Ops:
  0.6 26.6 %copy-start = (f32[4,4,32,180]{3,2,1,0:T(8,128)S(1)}, f32[4,4,32,180]{3,2,1,0:T(8,128)}, u32[]{:S(2)}) copy-start(f32[4,4,32,180]{3,2,1,0:T(8,128)} %param.6) | copy-start | bytes 1105924
  0.6 18.6 %copy-start.10 = (s32[256]{0:T(256)S(1)}, s32[256]{0:T(256)}, u32[]{:S(2)}) copy-start(s32[256]{0:T(256)} %param.8) | copy-start | bytes 3076
  2.4 27.0 %copy-start.2 = (f32[4,1,32,180]{3,2,1,0:T(8,128)}, f32[4,1,32,180]{3,2,1,0:T(8,128)S(1)}, u32[]{:S(2)}) copy-start(f32[4,1,32,180]{3,2,1,0:T(8,128)S(1)} %get-tuple-element.15) | copy-start | bytes 276484
  3.4 25.8 %collective-permute-start.3 = (f32[4,5,3,180]{3,2,1,0:T(4,128)S(1)}, f32[4,5,3,180]{3,2,1,0:T(4,128)S(1)}, u32[]{:S(2)}, u32[]{:S(2)}) collective-permute-start(f32[4,5,3,180]{3,2,1,0:T(4,128)S(1)} %get-tuple-element.9), channel_id=1, source_target_pairs={{4,0},{8,4},{12,8},{16,12},{20,16},{24,20},{28,24},{5,1},{9,5},{13... | collective-permute-start | bytes 129608 | tf_op jit(solution)/shard_map/ppermute | solution.py:19
  4.7 24.5 %collective-permute-start.2 = (f32[4,5,3,180]{3,2,1,0:T(4,128)S(1)}, f32[4,5,3,180]{3,2,1,0:T(4,128)S(1)}, u32[]{:S(2)}, u32[]{:S(2)}) collective-permute-start(f32[4,5,3,180]{3,2,1,0:T(4,128)S(1)} %get-tuple-element.8), channel_id=1, source_target_pairs={{0,4},{4,8},{8,12},{12,16},{16,20},{20,24},{24,28},{1,5},{5,9},{9,... | collective-permute-start | bytes 129608 | tf_op jit(solution)/shard_map/ppermute | solution.py:17
  8.9 11.7 %collective-permute-start.1 = (f32[4,4,32,3]{3,2,1,0:T(8,128)S(1)}, f32[4,4,32,3]{3,2,1,0:T(8,128)S(1)}, u32[]{:S(2)}, u32[]{:S(2)}) collective-permute-start(f32[4,4,32,3]{3,2,1,0:T(8,128)S(1)} %get-tuple-element.13), channel_id=1, source_target_pairs={{1,0},{2,1},{3,2},{0,3},{5,4},{6,5},{7,6},{4,7},{9,8},{10,9},{11,1... | collective-permute-start | bytes 18440 | tf_op jit(solution)/shard_map/ppermute | solution.py:19
  14.1 13.2 %collective-permute-start = (f32[4,4,32,3]{3,2,1,0:T(8,128)S(1)}, f32[4,4,32,3]{3,2,1,0:T(8,128)S(1)}, u32[]{:S(2)}, u32[]{:S(2)}) collective-permute-start(f32[4,4,32,3]{3,2,1,0:T(8,128)S(1)} %get-tuple-element.12), channel_id=1, source_target_pairs={{0,1},{1,2},{2,3},{3,0},{4,5},{5,6},{6,7},{7,4},{8,9},{9,10},{10,1... | collective-permute-start | bytes 18440 | tf_op jit(solution)/shard_map/ppermute | solution.py:17
  14.1 19.5 %all-to-all-start = ((f32[4,32,180]{2,1,0:T(8,128)}), f32[4,32,180]{2,1,0:T(8,128)}, u32[]{:S(2)}, u32[]{:S(2)}) async-start(f32[4,32,180]{2,1,0:T(8,128)} %get-tuple-element.14), calls=%async_computation | async-start | bytes 262144 | tf_op jit(solution)/shard_map/all_to_all | solution.py:156
  29.2 0.6 %copy-start.6 = (f32[4,5,3,180]{3,2,1,0:T(4,128)}, f32[4,5,3,180]{3,2,1,0:T(4,128)S(1)}, u32[]{:S(2)}) copy-start(f32[4,5,3,180]{3,2,1,0:T(4,128)S(1)} %collective-permute-done.2) | copy-start | bytes 129604
  30.1 0.9 %copy-start.3 = (f32[4,1,32,180]{3,2,1,0:T(8,128)S(1)}, f32[4,1,32,180]{3,2,1,0:T(8,128)}, u32[]{:S(2)}) copy-start(f32[4,1,32,180]{3,2,1,0:T(8,128)} %copy-done.2) | copy-start | bytes 276484
  30.1 0.9 %copy-start.7 = (f32[4,5,3,180]{3,2,1,0:T(4,128)S(1)}, f32[4,5,3,180]{3,2,1,0:T(4,128)}, u32[]{:S(2)}) copy-start(f32[4,5,3,180]{3,2,1,0:T(4,128)} %copy-done.6) | copy-start | bytes 129604
  30.1 7.7 %copy-start.8 = (s32[720]{0:T(1024)S(1)}, s32[720]{0:T(1024)}, u32[]{:S(2)}) copy-start(s32[720]{0:T(1024)} %constant.16.clone) | copy-start | bytes 8644
  36.9 3.9 %copy-start.4 = (f32[720,721]{1,0:T(8,128)S(1)}, f32[720,721]{1,0:T(8,128)}, u32[]{:S(2)}) copy-start(f32[720,721]{1,0:T(8,128)} %constant.15.clone) | copy-start | bytes 6229444
  36.9 3.9 %copy-start.5 = (f32[32,720]{1,0:T(8,128)S(1)}, f32[32,720]{1,0:T(8,128)}, u32[]{:S(2)}) copy-start(f32[32,720]{1,0:T(8,128)} %all_to_all.26) | copy-start | bytes 276484
  42.9 10.6 %all-to-all-start.1 = ((f32[4,32,181]{2,1,0:T(8,128)}), f32[4,32,181]{2,1,0:T(8,128)}, u32[]{:S(2)}, u32[]{:S(2)}) async-start(f32[4,32,181]{2,1,0:T(8,128)} %pad_maximum_fusion.7), calls=%async_computation.1 | async-start | bytes 262144 | tf_op jit(solution)/shard_map/all_to_all | solution.py:171
  55.2 3.7 %copy-start.1 = (f32[4,4,33,180]{3,2,1,0:T(8,128)S(1)}, f32[4,4,33,180]{3,2,1,0:T(8,128)}, u32[]{:S(2)}) copy-start(f32[4,4,33,180]{3,2,1,0:T(8,128)} %fusion.6) | copy-start | bytes 1140484
  55.2 3.7 %copy-start.9 = (f32[32]{0:T(128)S(1)}, f32[32]{0:T(128)}, u32[]{:S(2)}) copy-start(f32[32]{0:T(128)} %fusion.33) | copy-start | bytes 388
where the time goes:
time: 60.6 us; the launch traced here: 59.9 us
  starting transfers between devices  18.5 us (31%)
  other arithmetic  14.5 us (24%)
  waiting for transfers between devices  11.4 us (19%)
  local copies, waits for them, and re-layouts  10.3 us (17%)
  matrix products  4.33 us (7%)
  between operations  0.84 us (1%)
    ppermute x2, waiting for transfers between devices, padded(): lax.ppermute(tail, axis, [(i, (i + 1) % count) for i in range(ends)])  6.58 us
    ppermute x2, starting transfers between devices, padded(): lax.ppermute(head, axis, [((i + 1) % count, i) for i in range(ends)])  6.42 us
    all_to_all x1, starting transfers between devices, circle_filter(): lax.all_to_all(row_block, 'lon', split_axis=0, concat_axis=1, tiled=True)  5.09 us
    all_to_all x3, local copies, waits for them, and re-layouts, circle_filter(): lax.all_to_all(row_block, 'lon', split_axis=0, concat_axis=1, tiled=True)  5.04 us
    all_to_all x1, waiting for transfers between devices, circle_filter(): back = lax.all_to_all(slabs, 'lon', split_axis=0, concat_axis=1, tiled=True)  4.23 us
    all_to_all x1, starting transfers between devices, circle_filter(): back = lax.all_to_all(slabs, 'lon', split_axis=0, concat_axis=1, tiled=True)  3.95 us
    ppermute x2, starting transfers between devices, padded(): lax.ppermute(tail, axis, [(i, (i + 1) % count) for i in range(ends)])  3.04 us
    dot_general x1, matrix products, dense_lowpass(): coeff = jnp.dot(row_block, forward, precision=highest)  2.97 us
  transfers between devices with their start and end apart: 6, of which 3 were waited for; matrix products, arithmetic and copies ran while one was open for 16% of the time, Pallas kernels for 0%

commit v1 on v0

--- a/solution.py
+++ b/solution.py
@@ -4,6 +4,28 @@
 import jax.numpy as jnp
 from jax import lax
 from jax.sharding import PartitionSpec as P
+
+
+def show_chains(m, link_axis):
+    work_now = lax.axis_size(link_axis)
+    t1 = lax.axis_index(link_axis)
+    part_now, mid_arr = (work_now, t1)
+    b_now = m.shape[0] // part_now
+    met_up = list(m.shape)
+    met_up[0] = b_now
+    odd = met_up[1]
+    met_up[1] = odd * part_now
+    base_arr = jnp.zeros(met_up, m.dtype)
+    for kk in range(part_now):
+        p_next = lax.dynamic_slice_in_dim(m, (mid_arr ^ kk) * b_now, b_now, axis=0)
+        if kk:
+            p_next = lax.ppermute(
+                p_next,
+                axis_name=link_axis,
+                perm=[(hop_no, hop_no ^ kk) for hop_no in range(part_now)],
+            )
+        base_arr = lax.dynamic_update_slice_in_dim(base_arr, p_next, (mid_arr ^ kk) * odd, axis=1)
+    return base_arr
 
 
 def padded(cells, sides, width, closed):
@@ -168,7 +190,7 @@
         [lowpass_ext[:, k * block_cols : (k + 1) * block_cols + 1] for k in range(lon_groups)],
         axis=0,
     )
-    back = lax.all_to_all(slabs, "lon", split_axis=0, concat_axis=1, tiled=True)
+    back = show_chains(slabs, link_axis="lon")
     return back.reshape(row_count, block_cols + 1)
 
 

time: 60.6 us -> 53.7 us (0.89)
  other arithmetic: 14.5 us -> 7.76 us
    ppermute x0 -> x3, starting transfers between devices: none -> 4.52 us  [show_chains(): lax.ppermute(p_next, axis_name=link_axis, perm=[(hop_no, hop_no ^ kk) for...]
    all_to_all x1 -> x0, waiting for transfers between devices: 4.23 us -> none  [circle_filter(): back = lax.all_to_all(slabs, 'lon', split_axis=0, concat_axis=1, tiled=True)]
    all_to_all x1 -> x0, starting transfers between devices: 3.95 us -> none  [circle_filter(): back = lax.all_to_all(slabs, 'lon', split_axis=0, concat_axis=1, tiled=True)]
    ppermute x0 -> x3, waiting for transfers between devices: none -> 3.95 us  [show_chains(): lax.ppermute(p_next, axis_name=link_axis, perm=[(hop_no, hop_no ^ kk) for...]
    mul x1, other arithmetic: 2.4 us -> 0.42 us  [body(): ppm_flux(lat_ext[:, :tracer_count], lat_ext[:, tracer_count:, 2:lat_rows...]
    mul x2, other arithmetic: 2.74 us -> 0.83 us  [ppm_flux(): 0.5 * courant_faces]
    mul x1, other arithmetic: 1.76 us -> 0.5 us  [ppm_flux(): return courant_faces * jnp.where(courant_faces > 0, upwind, downwind)]
    gt x1, other arithmetic: 0.93 us -> 0.02 us  [ppm_flux(): return courant_faces * jnp.where(courant_faces > 0, upwind, downwind)]
  transfers between devices with their start and end apart: 6 -> 8, of which waited for: 3 -> 4; matrix products, arithmetic and copies ran while one was open for 16% -> 12% of each run, Pallas kernels for 0% -> 0%
where the time goes in v1:
time: 53.7 us; the launch traced here: 53.3 us
  starting transfers between devices  19.1 us (36%)
  waiting for transfers between devices  11.1 us (21%)
  local copies, waits for them, and re-layouts  10.1 us (19%)
  other arithmetic  7.76 us (14%)
  matrix products  4.33 us (8%)
  between operations  0.92 us (2%)
    ppermute x2, waiting for transfers between devices, padded(): lax.ppermute(tail, axis, [(i, (i + 1) % count) for i in range(ends)])  6.58 us
    ppermute x2, starting transfers between devices, padded(): lax.ppermute(head, axis, [((i + 1) % count, i) for i in range(ends)])  6.42 us
    all_to_all x1, starting transfers between devices, circle_filter(): lax.all_to_all(row_block, 'lon', split_axis=0, concat_axis=1, tiled=True)  5.09 us
    all_to_all x3, local copies, waits for them, and re-layouts, circle_filter(): lax.all_to_all(row_block, 'lon', split_axis=0, concat_axis=1, tiled=True)  5.02 us
    ppermute x3, starting transfers between devices, show_chains(): lax.ppermute(p_next, axis_name=link_axis, perm=[(hop_no, hop_no ^ kk) for...  4.52 us
    ppermute x3, waiting for transfers between devices, show_chains(): lax.ppermute(p_next, axis_name=link_axis, perm=[(hop_no, hop_no ^ kk) for...  3.95 us
    ppermute x2, starting transfers between devices, padded(): lax.ppermute(tail, axis, [(i, (i + 1) % count) for i in range(ends)])  3.04 us
    dot_general x1, matrix products, dense_lowpass(): coeff = jnp.dot(row_block, forward, precision=highest)  2.97 us
  transfers between devices with their start and end apart: 8, of which 4 were waited for; matrix products, arithmetic and copies ran while one was open for 12% of the time, Pallas kernels for 0%

profile of v1, /device:TPU:0, one launch (start us, length us, event | category | flops | bytes accessed | tf_op | source)
XLA Modules:
  0.0 53.3 jit_solution(266942657313929172)
XLA Ops:
  0.6 0.0 copy-start
  0.7 1.7 %slice_bitcast_fusion.2 = (f32[4,32,180]{2,1,0:T(8,128)}, f32[4,1,32,180]{3,2,1,0:T(8,128)S(1)}) fusion(f32[2,4,32,180]{3,2,1,0:T(8,128)} %param.7), kind=kLoop, calls=%fused_computation.59 | loop fusion | bytes 368640 | tf_op jit(solution)/shard_map/all_to_all | solution.py:178
  2.4 1.1 %pad_maximum_fusion.9 = (f32[4,5,3,180]{3,2,1,0:T(4,128)S(1)}, f32[4,5,3,180]{3,2,1,0:T(4,128)S(1)}) fusion(f32[4,1,32,180]{3,2,1,0:T(8,128)S(1)} %get-tuple-element.15, f32[4,4,32,180]{3,2,1,0:T(8,128)} %param.6), kind=kLoop, calls=%fused_computation.63 | loop fusion | flops 21600 | bytes 547200 | tf_op jit(solution)/shard_map/slice | solution.py:36
  3.4 1.3 %collective-permute-start.6 = (f32[4,5,3,180]{3,2,1,0:T(4,128)S(1)}, f32[4,5,3,180]{3,2,1,0:T(4,128)S(1)}, u32[]{:S(2)}, u32[]{:S(2)}) collective-permute-start(f32[4,5,3,180]{3,2,1,0:T(4,128)S(1)} %get-tuple-element.9), channel_id=1, source_target_pairs={{4,0},{8,4},{12,8},{16,12},{20,16},{24,20},{28,24},{5,1},{9,5},{13... | collective-permute-start | bytes 129608 | tf_op jit(solution)/shard_map/ppermute | solution.py:41
  4.7 3.0 %collective-permute-start.5 = (f32[4,5,3,180]{3,2,1,0:T(4,128)S(1)}, f32[4,5,3,180]{3,2,1,0:T(4,128)S(1)}, u32[]{:S(2)}, u32[]{:S(2)}) collective-permute-start(f32[4,5,3,180]{3,2,1,0:T(4,128)S(1)} %get-tuple-element.8), channel_id=1, source_target_pairs={{0,4},{4,8},{8,12},{12,16},{16,20},{20,24},{24,28},{1,5},{5,9},{9,... | collective-permute-start | bytes 129608 | tf_op jit(solution)/shard_map/ppermute | solution.py:39
  7.8 1.2 %fusion.34 = (f32[4,4,32,3]{3,2,1,0:T(8,128)S(1)}, f32[4,4,32,3]{3,2,1,0:T(8,128)S(1)}) fusion(f32[4,4,32,180]{3,2,1,0:T(8,128)} %param.6), kind=kLoop, calls=%fused_computation.84 | loop fusion | bytes 24576 | tf_op jit(solution)/shard_map/slice | solution.py:36
  8.9 5.1 %collective-permute-start.4 = (f32[4,4,32,3]{3,2,1,0:T(8,128)S(1)}, f32[4,4,32,3]{3,2,1,0:T(8,128)S(1)}, u32[]{:S(2)}, u32[]{:S(2)}) collective-permute-start(f32[4,4,32,3]{3,2,1,0:T(8,128)S(1)} %get-tuple-element.13), channel_id=1, source_target_pairs={{1,0},{2,1},{3,2},{0,3},{5,4},{6,5},{7,6},{4,7},{9,8},{10,9},{11,1... | collective-permute-start | bytes 18440 | tf_op jit(solution)/shard_map/ppermute | solution.py:41
  14.1 0.0 collective-permute-start.3
  14.1 5.1 %all-to-all-start = ((f32[4,32,180]{2,1,0:T(8,128)}), f32[4,32,180]{2,1,0:T(8,128)}, u32[]{:S(2)}, u32[]{:S(2)}) async-start(f32[4,32,180]{2,1,0:T(8,128)} %get-tuple-element.14), calls=%async_computation | async-start | bytes 262144 | tf_op jit(solution)/shard_map/all_to_all | solution.py:178
  19.2 0.1 dynamic_slice.18
  19.3 0.1 tile.10
  19.4 0.1 broadcast_compare_fusion.1
  19.5 0.6 %fusion.33 = f32[32]{0:T(128)} fusion(s32[]{:T(128)S(6)} %mul.208), kind=kLoop, calls=%fused_computation.81 | loop fusion | flops 192 | bytes 132 | tf_op jit(solution)/shard_map/sin | solution.py:83
  20.0 0.6 %collective-permute-done.4 = f32[4,4,32,3]{3,2,1,0:T(8,128)S(1)} collective-permute-done((f32[4,4,32,3]{3,2,1,0:T(8,128)S(1)}, f32[4,4,32,3]{3,2,1,0:T(8,128)S(1)}, u32[]{:S(2)}, u32[]{:S(2)}) %collective-permute-start.4) | collective-permute-done | bytes 6176 | tf_op jit(solution)/shard_map/ppermute | solution.py:41
  20.7 6.6 %collective-permute-done.3 = f32[4,4,32,3]{3,2,1,0:T(8,128)S(1)} collective-permute-done((f32[4,4,32,3]{3,2,1,0:T(8,128)S(1)}, f32[4,4,32,3]{3,2,1,0:T(8,128)S(1)}, u32[]{:S(2)}, u32[]{:S(2)}) %collective-permute-start.3) | collective-permute-done | bytes 6176 | tf_op jit(solution)/shard_map/ppermute | solution.py:39
  27.2 0.3 pad_maximum_fusion.5
  27.5 0.5 %fusion.28 = f32[4,4,32,183]{3,2,1,0:T(8,128)S(1)} fusion(f32[4,4,32,186]{3,2,1,0:T(8,128)S(1)} %pad_maximum_fusion.5, f32[4,4,32,180]{3,2,1,0:T(8,128)S(1)} %copy-done, f32[4,4,32,3]{3,2,1,0:T(8,128)S(1)} %collective-permute-done.3, f32[4,4,32,3]{3,2,1,0:T(8,128)S(1)} %collective-permute-done.4), kind=kLoop, calls=%fused_computation.46 | loop fusion | flops 655872 | bytes 1505280 | tf_op jit(solution)/shard_map/sub | solution.py:54
  28.1 1.1 %slice_subtract_fusion.3 = (f32[4,4,32,182]{3,2,1,0:T(8,128)S(1)}, f32[4,4,32,182]{3,2,1,0:T(8,128)}) fusion(f32[4,4,32,183]{3,2,1,0:T(8,128)S(1)} %fusion.28, f32[4,4,32,186]{3,2,1,0:T(8,128)S(1)} %pad_maximum_fusion.5), kind=kLoop, calls=%fused_computation.50 | loop fusion | flops 465920 | bytes 1863680 | tf_op jit(solution)/shard_map/sub | solution.py:64
  29.2 0.0 collective-permute-done.6
  29.2 0.0 collective-permute-done.5
  29.2 0.1 pad_maximum_fusion
  29.3 0.5 copy-done.8
  29.8 0.3 fusion.13
  30.1 0.0 copy-start.14
  30.1 0.2 slice_subtract_fusion
  30.3 0.7 %copy-done.3 = f32[4,1,32,180]{3,2,1,0:T(8,128)S(1)} copy-done((f32[4,1,32,180]{3,2,1,0:T(8,128)S(1)}, f32[4,1,32,180]{3,2,1,0:T(8,128)}, u32[]{:S(2)}) %copy-start.3) | copy-done | bytes 92184
  31.0 0.0 copy-done.9
  31.0 0.7 %compare_bitcast_fusion = (pred[4,33,180]{2,1,0:T(8,128)(4,1)}, f32[4,1,33,180]{3,2,1,0:T(8,128)S(1)}) fusion(f32[4,1,32,180]{3,2,1,0:T(8,128)S(1)} %copy-done.3, f32[4,4,32,180]{3,2,1,0:T(8,128)S(1)} %copy-done, f32[4,5,3,180]{3,2,1,0:T(4,128)S(1)} %copy-done.9), kind=kLoop, calls=%fused_computation.55 | loop fusion | flops 71280 | bytes 622800 | tf_op jit(solution)/shard_map/jit(_where)/broadcast_in_dim | solution.py:74
  31.7 0.7 %copy-done.5 = f32[4,1,33,180]{3,2,1,0:T(8,128)} copy-done((f32[4,1,33,180]{3,2,1,0:T(8,128)}, f32[4,1,33,180]{3,2,1,0:T(8,128)S(1)}, u32[]{:S(2)}) %copy-start.5) | copy-done | bytes 95064
  32.4 0.8 %multiply_bitcast_fusion = (f32[4,33,180]{2,1,0:T(8,128)}, f32[4,33,180]{2,1,0:T(8,128)}, f32[4,33,180]{2,1,0:T(8,128)}) fusion(f32[4,1,33,180]{3,2,1,0:T(8,128)S(1)} %get-tuple-element.5), kind=kLoop, calls=%fused_computation.54 | loop fusion | flops 95040 | bytes 380160 | tf_op jit(solution)/shard_map/mul | solution.py:66
  33.2 0.0 all-to-all-done
  33.2 1.6 %copy.8 = f32[32,4,180]{2,1,0:T(4,128)} copy(f32[32,4,180]{2,0,1:T(8,128)} %bitcast.1) | data formatting | bytes 184320 | tf_op jit(solution)/shard_map/all_to_all | solution.py:178
  34.8 1.7 %all_to_all.17 = f32[32,720]{1,0:T(8,128)} reshape(f32[32,4,180]{2,1,0:T(4,128)} %copy.8) | data formatting | bytes 184320 | tf_op jit(solution)/shard_map/all_to_all | solution.py:178
  36.5 0.9 %slice.175 = f32[32,1]{1,0:T(8,128)S(1)} slice(f32[32,720]{1,0:T(8,128)} %all_to_all.17), slice={[0:32], [719:720]} | slice | bytes 256 | tf_op jit(solution)/shard_map/slice | solution.py:182
  37.4 3.0 %fusion = f32[32,720]{1,0:T(8,128)S(1)} fusion(f32[720,720]{1,0:T(8,128)} %constant.15.clone, f32[32,720]{1,0:T(8,128)} %all_to_all.17, s32[720]{0:T(1024)S(1)} %copy-done.14, s32[32]{0:T(128)S(1)} %get-tuple-element.3), kind=kOutput, calls=%fused_computation.2 | convolution fusion | flops 199111680 | bytes 2260928 | tf_op jit(solution)/shard_map/dot_general | solution.py:171
  40.5 1.4 %convolution_select_fusion = f32[32,721]{1,0:T(8,128)S(1)} fusion(f32[32,720]{1,0:T(8,128)S(1)} %fusion, f32[720,721]{1,0:T(8,128)S(1)} %copy-done.4, f32[32,720]{1,0:T(8,128)S(1)} %copy-done.7, f32[32,1]{1,0:T(8,128)S(1)} %slice.175, pred[32]{0:T(512)(128)(4,1)S(1)} %get-tuple-element.2), kind=kOutput, calls=%fused_computation | convolution fusion | flops 199388224 | bytes 2353248 | tf_op jit(solution)/shard_map/dot_general | solution.py:173
  41.8 0.1 slice_bitcast_fusion.6
  42.0 1.6 %collective-permute-start = (f32[1,32,181]{2,1,0:T(8,128)S(1)}, f32[1,32,181]{2,1,0:T(8,128)S(1)}, u32[]{:S(2)}, u32[]{:S(2)}) collective-permute-start(f32[1,32,181]{2,1,0:T(8,128)S(1)} %get-tuple-element.24), channel_id=1, source_target_pairs={{0,1},{1,0},{2,3},{3,2},{4,5},{5,4},{6,7},{7,6},{8,9},{9,8},{10,11... | collective-permute-start | bytes 69512 | tf_op jit(solution)/shard_map/ppermute | solution.py:22
  43.6 0.0 copy-start.1
  43.6 0.4 fusion.6
  44.1 1.2 %collective-permute-start.1 = (f32[1,32,181]{2,1,0:T(8,128)S(1)}, f32[1,32,181]{2,1,0:T(8,128)S(1)}, u32[]{:S(2)}, u32[]{:S(2)}) collective-permute-start(f32[1,32,181]{2,1,0:T(8,128)S(1)} %get-tuple-element.23), channel_id=1, source_target_pairs={{0,2},{1,3},{2,0},{3,1},{4,6},{5,7},{6,4},{7,5},{8,10},{9,11},{10,... | collective-permute-start | bytes 69512 | tf_op jit(solution)/shard_map/ppermute | solution.py:22
  45.2 1.8 %collective-permute-start.2 = (f32[1,32,181]{2,1,0:T(8,128)S(1)}, f32[1,32,181]{2,1,0:T(8,128)S(1)}, u32[]{:S(2)}, u32[]{:S(2)}) collective-permute-start(f32[1,32,181]{2,1,0:T(8,128)S(1)} %get-tuple-element.22), channel_id=1, source_target_pairs={{0,3},{1,2},{2,1},{3,0},{4,7},{5,6},{6,5},{7,4},{8,11},{9,10},{10,... | collective-permute-start | bytes 69512 | tf_op jit(solution)/shard_map/ppermute | solution.py:22
  47.0 0.0 collective-permute-done
  47.0 2.8 %collective-permute-done.1 = f32[1,32,181]{2,1,0:T(8,128)S(1)} collective-permute-done((f32[1,32,181]{2,1,0:T(8,128)S(1)}, f32[1,32,181]{2,1,0:T(8,128)S(1)}, u32[]{:S(2)}, u32[]{:S(2)}) %collective-permute-start.1) | collective-permute-done | bytes 23200 | tf_op jit(solution)/shard_map/ppermute | solution.py:22
  49.8 1.1 %collective-permute-done.2 = f32[1,32,181]{2,1,0:T(8,128)S(1)} collective-permute-done((f32[1,32,181]{2,1,0:T(8,128)S(1)}, f32[1,32,181]{2,1,0:T(8,128)S(1)}, u32[]{:S(2)}, u32[]{:S(2)}) %collective-permute-start.2) | collective-permute-done | bytes 23200 | tf_op jit(solution)/shard_map/ppermute | solution.py:22
  51.0 0.8 %slice_bitcast_fusion = f32[4,32,180]{2,1,0:T(8,128)} fusion(f32[4,1,32,181]{3,2,0,1:T(8,128)S(1)} %bitcast.36), kind=kLoop, calls=%fused_computation.56 | loop fusion | bytes 184320 | tf_op jit(solution)/shard_map/squeeze | solution.py:213
  51.8 0.5 fusion.22
  52.3 1.0 %fusion.17 = f32[4,4,32,180]{3,2,1,0:T(8,128)} fusion(f32[4,4,32,180]{3,2,1,0:T(8,128)S(1)} %copy-done, f32[4,4,33,180]{3,2,1,0:T(8,128)S(1)} %fusion.6, f32[4,4,32,181]{3,2,1,0:T(8,128)S(1)} %fusion.22, f32[32]{0:T(128)S(1)} %copy-done.15), kind=kLoop, calls=%fused_computation.30 | loop fusion | flops 460800 | bytes 2211968 | tf_op jit(solution)/shard_map/sub | solution.py:225
  (37 shorter events, 0.2 us)
Async XLA Ops:
  0.6 26.6 %copy-start = (f32[4,4,32,180]{3,2,1,0:T(8,128)S(1)}, f32[4,4,32,180]{3,2,1,0:T(8,128)}, u32[]{:S(2)}) copy-start(f32[4,4,32,180]{3,2,1,0:T(8,128)} %param.6) | copy-start | bytes 1105924
  0.6 18.6 %copy-start.16 = (s32[256]{0:T(256)S(1)}, s32[256]{0:T(256)}, u32[]{:S(2)}) copy-start(s32[256]{0:T(256)} %param.8) | copy-start | bytes 3076
  2.4 27.0 %copy-start.2 = (f32[4,1,32,180]{3,2,1,0:T(8,128)}, f32[4,1,32,180]{3,2,1,0:T(8,128)S(1)}, u32[]{:S(2)}) copy-start(f32[4,1,32,180]{3,2,1,0:T(8,128)S(1)} %get-tuple-element.15) | copy-start | bytes 276484
  3.4 25.8 %collective-permute-start.6 = (f32[4,5,3,180]{3,2,1,0:T(4,128)S(1)}, f32[4,5,3,180]{3,2,1,0:T(4,128)S(1)}, u32[]{:S(2)}, u32[]{:S(2)}) collective-permute-start(f32[4,5,3,180]{3,2,1,0:T(4,128)S(1)} %get-tuple-element.9), channel_id=1, source_target_pairs={{4,0},{8,4},{12,8},{16,12},{20,16},{24,20},{28,24},{5,1},{9,5},{13... | collective-permute-start | bytes 129608 | tf_op jit(solution)/shard_map/ppermute | solution.py:41
  4.7 24.5 %collective-permute-start.5 = (f32[4,5,3,180]{3,2,1,0:T(4,128)S(1)}, f32[4,5,3,180]{3,2,1,0:T(4,128)S(1)}, u32[]{:S(2)}, u32[]{:S(2)}) collective-permute-start(f32[4,5,3,180]{3,2,1,0:T(4,128)S(1)} %get-tuple-element.8), channel_id=1, source_target_pairs={{0,4},{4,8},{8,12},{12,16},{16,20},{20,24},{24,28},{1,5},{5,9},{9,... | collective-permute-start | bytes 129608 | tf_op jit(solution)/shard_map/ppermute | solution.py:39
  8.9 11.7 %collective-permute-start.4 = (f32[4,4,32,3]{3,2,1,0:T(8,128)S(1)}, f32[4,4,32,3]{3,2,1,0:T(8,128)S(1)}, u32[]{:S(2)}, u32[]{:S(2)}) collective-permute-start(f32[4,4,32,3]{3,2,1,0:T(8,128)S(1)} %get-tuple-element.13), channel_id=1, source_target_pairs={{1,0},{2,1},{3,2},{0,3},{5,4},{6,5},{7,6},{4,7},{9,8},{10,9},{11,1... | collective-permute-start | bytes 18440 | tf_op jit(solution)/shard_map/ppermute | solution.py:41
  14.1 13.2 %collective-permute-start.3 = (f32[4,4,32,3]{3,2,1,0:T(8,128)S(1)}, f32[4,4,32,3]{3,2,1,0:T(8,128)S(1)}, u32[]{:S(2)}, u32[]{:S(2)}) collective-permute-start(f32[4,4,32,3]{3,2,1,0:T(8,128)S(1)} %get-tuple-element.12), channel_id=1, source_target_pairs={{0,1},{1,2},{2,3},{3,0},{4,5},{5,6},{6,7},{7,4},{8,9},{9,10},{10,1... | collective-permute-start | bytes 18440 | tf_op jit(solution)/shard_map/ppermute | solution.py:39
  14.1 19.1 %all-to-all-start = ((f32[4,32,180]{2,1,0:T(8,128)}), f32[4,32,180]{2,1,0:T(8,128)}, u32[]{:S(2)}, u32[]{:S(2)}) async-start(f32[4,32,180]{2,1,0:T(8,128)} %get-tuple-element.14), calls=%async_computation | async-start | bytes 262144 | tf_op jit(solution)/shard_map/all_to_all | solution.py:178
  29.2 0.6 %copy-start.8 = (f32[4,5,3,180]{3,2,1,0:T(4,128)}, f32[4,5,3,180]{3,2,1,0:T(4,128)S(1)}, u32[]{:S(2)}) copy-start(f32[4,5,3,180]{3,2,1,0:T(4,128)S(1)} %collective-permute-done.5) | copy-start | bytes 129604
  30.1 0.9 %copy-start.3 = (f32[4,1,32,180]{3,2,1,0:T(8,128)S(1)}, f32[4,1,32,180]{3,2,1,0:T(8,128)}, u32[]{:S(2)}) copy-start(f32[4,1,32,180]{3,2,1,0:T(8,128)} %copy-done.2) | copy-start | bytes 276484
  30.1 0.9 %copy-start.9 = (f32[4,5,3,180]{3,2,1,0:T(4,128)S(1)}, f32[4,5,3,180]{3,2,1,0:T(4,128)}, u32[]{:S(2)}) copy-start(f32[4,5,3,180]{3,2,1,0:T(4,128)} %copy-done.8) | copy-start | bytes 129604
  30.1 7.3 %copy-start.14 = (s32[720]{0:T(1024)S(1)}, s32[720]{0:T(1024)}, u32[]{:S(2)}) copy-start(s32[720]{0:T(1024)} %constant.17.clone) | copy-start | bytes 8644
  31.7 0.7 %copy-start.5 = (f32[4,1,33,180]{3,2,1,0:T(8,128)}, f32[4,1,33,180]{3,2,1,0:T(8,128)S(1)}, u32[]{:S(2)}) copy-start(f32[4,1,33,180]{3,2,1,0:T(8,128)S(1)} %get-tuple-element.5) | copy-start | bytes 285124
  36.5 4.0 %copy-start.4 = (f32[720,721]{1,0:T(8,128)S(1)}, f32[720,721]{1,0:T(8,128)}, u32[]{:S(2)}) copy-start(f32[720,721]{1,0:T(8,128)} %constant.16.clone) | copy-start | bytes 6229444
  36.5 4.0 %copy-start.7 = (f32[32,720]{1,0:T(8,128)S(1)}, f32[32,720]{1,0:T(8,128)}, u32[]{:S(2)}) copy-start(f32[32,720]{1,0:T(8,128)} %all_to_all.17) | copy-start | bytes 276484
  40.4 3.2 %copy-start.6 = (f32[4,1,33,180]{3,2,1,0:T(8,128)S(1)}, f32[4,1,33,180]{3,2,1,0:T(8,128)}, u32[]{:S(2)}) copy-start(f32[4,1,33,180]{3,2,1,0:T(8,128)} %copy-done.5) | copy-start | bytes 285124
  40.4 3.2 %copy-start.10 = (f32[4,33,180]{2,1,0:T(8,128)S(1)}, f32[4,33,180]{2,1,0:T(8,128)}, u32[]{:S(2)}) copy-start(f32[4,33,180]{2,1,0:T(8,128)} %get-tuple-element.16) | copy-start | bytes 285124
  40.4 3.2 %copy-start.11 = (f32[4,33,180]{2,1,0:T(8,128)S(1)}, f32[4,33,180]{2,1,0:T(8,128)}, u32[]{:S(2)}) copy-start(f32[4,33,180]{2,1,0:T(8,128)} %get-tuple-element.17) | copy-start | bytes 285124
  40.4 3.2 %copy-start.12 = (f32[4,33,180]{2,1,0:T(8,128)S(1)}, f32[4,33,180]{2,1,0:T(8,128)}, u32[]{:S(2)}) copy-start(f32[4,33,180]{2,1,0:T(8,128)} %get-tuple-element.18) | copy-start | bytes 285124
  40.5 3.2 %copy-start.13 = (pred[4,33,180]{2,1,0:T(8,128)(4,1)S(1)}, pred[4,33,180]{2,1,0:T(8,128)(4,1)}, u32[]{:S(2)}) copy-start(pred[4,33,180]{2,1,0:T(8,128)(4,1)} %get-tuple-element.4) | copy-start | bytes 71284
  42.0 5.0 %collective-permute-start = (f32[1,32,181]{2,1,0:T(8,128)S(1)}, f32[1,32,181]{2,1,0:T(8,128)S(1)}, u32[]{:S(2)}, u32[]{:S(2)}) collective-permute-start(f32[1,32,181]{2,1,0:T(8,128)S(1)} %get-tuple-element.24), channel_id=1, source_target_pairs={{0,1},{1,0},{2,3},{3,2},{4,5},{5,4},{6,7},{7,6},{8,9},{9,8},{10,11... | collective-permute-start | bytes 69512 | tf_op jit(solution)/shard_map/ppermute | solution.py:22
  43.6 8.2 %copy-start.1 = (f32[4,4,32,182]{3,2,1,0:T(8,128)S(1)}, f32[4,4,32,182]{3,2,1,0:T(8,128)}, u32[]{:S(2)}) copy-start(f32[4,4,32,182]{3,2,1,0:T(8,128)} %get-tuple-element.11) | copy-start | bytes 1118212
  44.1 5.8 %collective-permute-start.1 = (f32[1,32,181]{2,1,0:T(8,128)S(1)}, f32[1,32,181]{2,1,0:T(8,128)S(1)}, u32[]{:S(2)}, u32[]{:S(2)}) collective-permute-start(f32[1,32,181]{2,1,0:T(8,128)S(1)} %get-tuple-element.23), channel_id=1, source_target_pairs={{0,2},{1,3},{2,0},{3,1},{4,6},{5,7},{6,4},{7,5},{8,10},{9,11},{10,... | collective-permute-start | bytes 69512 | tf_op jit(solution)/shard_map/ppermute | solution.py:22
  45.2 5.7 %collective-permute-start.2 = (f32[1,32,181]{2,1,0:T(8,128)S(1)}, f32[1,32,181]{2,1,0:T(8,128)S(1)}, u32[]{:S(2)}, u32[]{:S(2)}) collective-permute-start(f32[1,32,181]{2,1,0:T(8,128)S(1)} %get-tuple-element.22), channel_id=1, source_target_pairs={{0,3},{1,2},{2,1},{3,0},{4,7},{5,6},{6,5},{7,4},{8,11},{9,10},{10,... | collective-permute-start | bytes 69512 | tf_op jit(solution)/shard_map/ppermute | solution.py:22
  51.0 1.3 %copy-start.15 = (f32[32]{0:T(128)S(1)}, f32[32]{0:T(128)}, u32[]{:S(2)}) copy-start(f32[32]{0:T(128)} %fusion.33) | copy-start | bytes 388
